TPU v7x, 256 devices: a whole 4x4x8 slice. The times are simulated.
256 devices in a mesh: grp: 4 (over y_lo, core), tm: 64 (over z, y_hi, x).
Axes of the slice: x: 4, y: 4 (y_hi: 2, y_lo: 2; y = y_hi * 2 + y_lo), z: 8, core: 2. Of those that a mesh axis runs over, the one named last changes fastest.
Arguments:
- records: bfloat16 [24576, 512], P('tm', 'grp'), may hold values from -6 to 6
- measured: bfloat16 [24576, 512], P('tm', 'grp'), may hold values from -6 to 6
- markov_params: float32 [64, 512, 512], P('tm', 'grp'), may hold values from -6 to 6
- seg_lengths: int32 [64], P('tm'), may hold values from 1 to 384, 15360 in all
Outputs:
- new_params: float32 [64, 512, 512], P('tm', 'grp')
- residual: bfloat16 [24576, 512], P('tm', 'grp')
Inputs may be any that keep to these rules, and one draw needn't show every extreme that they name: seg_lengths of all 64 segments sum to 15360; some segment is full.
All inputs are finite; a program needn't handle non-finite values. No bound on the sum of `seg_lengths` on one device may be relied on, other than what follows from the above.
Results may differ from a plain program's by a relative error of at most 0.0039.
Values may be sent and summed in bfloat16 or wider, within the bound.
A program may use at most 64 MiB of HBM per device.

v0:
```python
import math

import jax
import jax.numpy as jnp
from jax import lax
from jax.sharding import PartitionSpec as P

M = 512
LAGS = 64


def passed_along(x, axis, by):
    count = lax.axis_size(axis)
    pairs = [(i, i + by) for i in range(count) if 0 <= i + by < count]
    return lax.ppermute(x, axis, pairs)


def shifted(value, axis, steps):
    count = lax.axis_size(axis)
    pairs = [(source, (source + steps) % count) for source in range(count)]
    return lax.ppermute(value, axis, pairs)


def arrange(by_offset, group_index, group_count):
    stacked = jnp.stack(by_offset)
    source_order = (group_index - jnp.arange(group_count, dtype=jnp.int32)) % group_count
    placed = jnp.take(stacked, source_order, axis=0)
    placed = jnp.transpose(placed, (1, 0, 2))
    return placed.reshape(placed.shape[0], placed.shape[1] * placed.shape[2])


def on_device(records, measured, markov_params, seg_lengths):
    lag_span = LAGS - 1
    row_count = records.shape[0]
    prior_rows = passed_along(records[row_count - lag_span :], "tm", 1)
    own_ext = jnp.concatenate([prior_rows, records], axis=0)
    group_count = lax.axis_size("grp")
    group_index = lax.axis_index("grp")
    by_offset = [own_ext]
    current = own_ext
    for offset in range(1, group_count):
        current = shifted(current, "grp", 1)
        by_offset.append(current)
    joined = arrange(by_offset, group_index, group_count)
    weights = markov_params.astype(jnp.bfloat16)
    out_width = weights.shape[1]
    empty_sum = jnp.zeros((row_count, out_width), jnp.float32)
    lag_piece = lax.all_gather(weights, "tm", axis=0, tiled=True)

    def forward_one_lag(partial_sum, lag_item):
        lag_weight, offset = lag_item
        window = lax.dynamic_slice_in_dim(joined, lag_span - offset, row_count, 0)
        product = lax.dot_general(
            window, lag_weight, (((1,), (1,)), ((), ())), preferred_element_type=jnp.float32
        )
        return (partial_sum + product, None)

    offsets = jnp.arange(lag_piece.shape[0], dtype=jnp.int32)
    result, unused = lax.scan(forward_one_lag, empty_sum, (lag_piece, offsets))
    predicted = result * (1.0 / math.sqrt(LAGS * M))
    position = jnp.arange(row_count, dtype=jnp.int32)
    live_mask = position < seg_lengths[0]
    residual = jnp.where(live_mask[:, None], measured.astype(jnp.float32) - predicted, 0.0).astype(
        jnp.bfloat16
    )
    dir_scale = 1.0 / math.sqrt(row_count * lax.axis_size("tm"))
    local_lags = markov_params.shape[0]

    def lag_one_lag(offset):
        window = lax.dynamic_slice_in_dim(joined, lag_span - offset, row_count, 0)
        product = lax.dot_general(
            residual, window, (((0,), (0,)), ((), ())), preferred_element_type=jnp.float32
        )
        return product * dir_scale

    direction = lax.psum_scatter(
        lax.map(lag_one_lag, jnp.arange(lax.axis_size("tm") * local_lags, dtype=jnp.int32)),
        "tm",
        scatter_dimension=0,
        tiled=True,
    )
    new_params = markov_params + 0.5 * direction
    return (new_params, residual)


def solution(mesh):
    in_specs = (P("tm", "grp"), P("tm", "grp"), P("tm", "grp", None), P("tm"))
    out_specs = (P("tm", "grp", None), P("tm", "grp"))
    return jax.shard_map(
        on_device, mesh=mesh, in_specs=in_specs, out_specs=out_specs, check_vma=False
    )
```

profile of v0, /device:TPU:8, one launch (start us, length us, event | category | flops | bytes accessed | tf_op | source)
XLA Modules:
  0.0 966.8 jit_solution(10353209963255993437)
XLA Ops:
  7.2 1.6 convert_element_type.10
  9.6 3.4 collective-permute-start
  13.0 1.4 collective-permute-done
  15.5 4.4 collective-permute-done.1
  20.5 3.5 collective-permute-done.2
  24.1 4.2 collective-permute-done.3
  29.8 130.8 %all-gather.2.cloned.1.call-done = bf16[64,128,512]{2,1,0:T(8,128)(2,1)} async-done(((bf16[1,128,512]{2,1,0:T(8,128)(2,1)}), bf16[64,128,512]{2,1,0:T(8,128)(2,1)}) %all-gather.2.cloned.1.call-update) | async-done | bytes 8388624 | tf_op jit(solution)/shard_map/all_gather | solution.py:48
  160.6 199.2 %while.26 = (s32[]{:T(128)}, f32[384,128]{1,0:T(8,128)S(1)}, s32[64]{0:T(128)S(1)}, bf16[447,512]{1,0:T(8,128)(2,1)S(1)}, bf16[64,128,512]{2,1,0:T(8,128)(2,1)},...) while((s32[]{:T(128)}, f32[384,128]{1,0:T(8,128)S(1)}, s32[64]{0:T(128)S(1)}, ...), condition=%wide.region_1.2_spmd.clone, body=%wide.region_0.1_spmd.clone.sunk | while | flops 50429960 | bytes 918181 | solution.py:59
  165.6 1.2 convolution_add_fusion.2
  184.2 1.2 convolution_add_fusion.2
  202.9 1.2 convolution_add_fusion.2
  212.3 1.2 convolution_add_fusion.2
  221.6 1.2 convolution_add_fusion.2
  224.7 1.2 convolution_add_fusion.2
  230.9 1.2 convolution_add_fusion.2
  252.7 1.2 convolution_add_fusion.2
  274.5 1.2 convolution_add_fusion.2
  280.7 1.2 convolution_add_fusion.2
  302.5 1.2 convolution_add_fusion.2
  324.3 1.2 convolution_add_fusion.2
  352.3 1.2 convolution_add_fusion.2
  360.8 197.1 %while.25 = (s32[]{:T(128)}, f32[64,128,512]{2,1,0:T(8,128)}, s32[64]{0:T(128)S(1)}, bf16[447,512]{1,0:T(8,128)(2,1)S(1)}, bf16[384,128]{1,0:T(8,128)(2,1)S(1)},...) while((s32[]{:T(128)}, f32[64,128,512]{2,1,0:T(8,128)}, s32[64]{0:T(128)S(1)}, ...), condition=%wide.region_3.4_spmd, body=%wide.region_2.3_spmd.sunk | while | flops 50397188 | bytes 1802907 | solution.py:77
  557.9 400.4 %reduce-scatter.2.cloned.1.call-done = f32[1,128,512]{2,1,0:T(8,128)} async-done(((f32[64,128,512]{2,1,0:T(8,128)}), f32[1,128,512]{2,1,0:T(8,128)}) %reduce-scatter.2.cloned.1.call-update) | async-done | bytes 262160 | tf_op jit(solution)/shard_map/reduce_scatter | solution.py:76
  958.3 1.7 multiply_add_fusion
  (399 shorter events, 215.7 us)
Async XLA Ops:
  7.2 153.4 %all-gather.2.cloned.1.call-start = ((), (), s32[]{:S(2)}) async-start(), calls=%async_computation.1 | async-start | bytes 8519680 | tf_op jit(solution)/shard_map/all_gather | solution.py:48
  8.9 949.5 %reduce-scatter.2.cloned.1.call-start = ((), (), s32[]{:S(2)}) async-start(), calls=%async_computation.2 | async-start | bytes 17039360 | tf_op jit(solution)/shard_map/reduce_scatter | solution.py:76
  9.6 4.8 collective-permute-start
  15.4 4.5 collective-permute-start.1
  19.9 4.2 collective-permute-start.2
  24.1 4.2 collective-permute-start.3
  29.1 929.2 %copy-start.1 = (f32[1,128,512]{2,1,0:T(8,128)S(1)}, f32[1,128,512]{2,1,0:T(8,128)}, u32[]{:S(2)}) copy-start(f32[1,128,512]{2,1,0:T(8,128)} %param.10) | copy-start | bytes 786436
  557.9 402.2 %copy-start = (bf16[384,128]{1,0:T(8,128)(2,1)}, bf16[384,128]{1,0:T(8,128)(2,1)S(1)}, u32[]{:S(2)}) copy-start(bf16[384,128]{1,0:T(8,128)(2,1)S(1)} %get-tuple-element.295) | copy-start | bytes 294916
Sparse Core Ops, SparseCore 0:
  12.1 148.3 all-gather.1
  558.0 400.2 reduce-scatter.1
where the time goes:
time: 971 us; the launch traced here: 967 us
  waiting for transfers between devices  545 us (56%)
  loops' own time  169 us (17%)
  local copies, waits for them, and re-layouts  132 us (14%)
  matrix products  97.1 us (10%)
  between operations  14.8 us (2%)
    reduce_scatter x1, waiting for transfers between devices, on_device(): lax.psum_scatter(lax.map(lag_one_lag, jnp.arange(lax.axis_size('tm') * lo...  400 us
    all_gather x1, waiting for transfers between devices, on_device(): lag_piece = lax.all_gather(weights, 'tm', axis=0, tiled=True)  131 us
    another operation x1, loops' own time, on_device(): result, unused = lax.scan(forward_one_lag, empty_sum, (lag_piece, offsets))  85 us
    another operation x1, loops' own time, on_device(): lax.map(lag_one_lag, jnp.arange(lax.axis_size('tm') * local_lags, dtype=j...  84.3 us
    dot_general x64, matrix products, forward_one_lag(): lax.dot_general(window, lag_weight, (((1,), (1,)), ((), ())), preferred_e...  76.7 us
    dynamic_slice x128, local copies, waits for them, and re-layouts, on_device(): result, unused = lax.scan(forward_one_lag, empty_sum, (lag_piece, offsets))  74.8 us
    dynamic_update_slice x128, local copies, waits for them, and re-layouts, on_device(): lax.map(lag_one_lag, jnp.arange(lax.axis_size('tm') * local_lags, dtype=j...  55.1 us
    dot_general x64, matrix products, lag_one_lag(): lax.dot_general(residual, window, (((0,), (0,)), ((), ())), preferred_ele...  20.4 us
  transfers between devices with their start and end apart: 6, of which 6 were waited for; matrix products, arithmetic and copies ran while one was open for 0% of the time, Pallas kernels for 0%

commit v1 on v0

v1 whole, which is shorter than its diff:
```python
import math

import jax
import jax.numpy as jnp
from jax import lax
from jax.experimental import pallas as pl
from jax.experimental.pallas import tpu as pltpu
from jax.sharding import PartitionSpec as P

M = 512
LAGS = 64
BF = jnp.bfloat16
F32 = jnp.float32


def body(len_ref, rec_ref, meas_ref, par_ref, new_ref, res_ref, wsend, wbuf, xraw, xf, xpf, xs, lsend, lraw, mraw, mf,
         acc, csend, crecv, rall, rt, rout, rres, dall, dxs, dxr, gs, gr, fs, fr,
         sb1, rb1, sa, ra, sm, rm, sh, rh, sring, rring, spair, rpair, sc, rc, sr, rr, sdx, rdx, sg, rg, sf, rf):
    tm = lax.axis_index("tm")
    grp = lax.axis_index("grp")
    z = tm // 8
    yh = (tm // 4) % 2
    x = tm % 4
    yl = grp // 2
    core = grp % 2
    q = yl * 2 + yh

    def spread(j):
        return z * 8 + core * 4 + j, yl * 2 + yh

    def t_out(c):
        return z * 8 + (c % 2) * 4 + grp, (c // 2) * 2 + yh

    def t_in(j):
        return z * 8 + core * 4 + j, x

    def peer(j):
        return z * 8 + (j % 2) * 4 + x, (j // 2) * 2 + core

    def along(step):
        return lax.rem(z + step + 8, 8) * 8 + yh * 4 + x, grp

    partner = (tm, yl * 2 + 1 - core)
    ahead = (lax.rem(z + core, 8) * 8 + yh * 4 + x, yl * 2 + 1 - core)
    behind = (lax.rem(z + core + 7, 8) * 8 + yh * 4 + x, yl * 2 + 1 - core)

    def is_me(dev):
        return jnp.logical_and(dev[0] == tm, dev[1] == grp)

    def send(src, dst, ssem, rsem, dev):
        return pltpu.make_async_remote_copy(src_ref=src, dst_ref=dst, send_sem=ssem, recv_sem=rsem,
                                            device_id={"tm": dev[0], "grp": dev[1]},
                                            device_id_type=pl.DeviceIdType.MESH)

    def start_any(src, dst, ssem, rsem, dev):
        me = is_me(dev)

        @pl.when(me)
        def _():
            pltpu.make_async_copy(src, dst, rsem).start()

        @pl.when(jnp.logical_not(me))
        def _():
            send(src, dst, ssem, rsem, dev).start()

    def done_any(src, dst, ssem, rsem, dev):
        @pl.when(jnp.logical_not(is_me(dev)))
        def _():
            send(src, dst, ssem, rsem, dev).wait_send()

    def got(dst, ssem, rsem):
        send(dst, dst, ssem, rsem, partner).wait_recv()

    barrier = pltpu.get_barrier_semaphore()
    count = jnp.int32(0)
    friends = [spread(j) for j in range(4)] + [t_out(j) for j in range(4)] + [t_in(j) for j in range(4)]
    for dev in friends:
        other = jnp.logical_not(is_me(dev))
        count = count + other.astype(jnp.int32)

        @pl.when(other)
        def _():
            pl.semaphore_signal(barrier, inc=1, device_id={"tm": dev[0], "grp": dev[1]},
                                device_id_type=pl.DeviceIdType.MESH)
    sure = [peer(lax.rem(q + k, 4)) for k in (1, 2, 3)] + [along(1), along(-1), partner, ahead, behind]
    for dev in sure:
        pl.semaphore_signal(barrier, inc=1, device_id={"tm": dev[0], "grp": dev[1]},
                            device_id_type=pl.DeviceIdType.MESH)
    for c in range(4):
        wsend[c] = par_ref[:, c * 128:(c + 1) * 128].astype(BF)
    lsend[...] = jnp.full((8, 128), len_ref[0], jnp.int32).astype(F32)
    pl.semaphore_wait(barrier, count + len(sure))

    for c in range(4):
        start_any(wsend.at[c], wbuf.at[tm], sb1.at[c], rb1.at[x], t_out(c))
    own_rows = pl.ds(pl.multiple_of(64 + 384 * x, 64), 384)
    for j in range(4):
        start_any(rec_ref, xraw.at[own_rows], sa.at[j], ra.at[x], spread(j))
    start_any(meas_ref, mraw, sm.at[0], rm.at[0], t_out(x))
    start_any(lsend, lraw, sm.at[1], rm.at[1], t_out(x))

    def pair_lags(chunk, half, sub):
        return wbuf.at[pl.ds(lax.rem(chunk + 8, 8) * 8 + half * 4 + sub * 2, 2)]

    def ring_send(way, step, sub):
        chunk = z - step if way == 0 else z + step
        ref = pair_lags(chunk, core, sub)
        return send(ref, ref, sring.at[way, step, sub], rring.at[way, step, sub], along(1 if way == 0 else -1))

    def pair_send(chunk_slot, chunk, sub):
        ref = pair_lags(chunk, core, sub)
        return send(ref, ref, spair.at[chunk_slot, sub], rpair.at[chunk_slot, sub], partner)

    def ring_got(way, step, sub):
        chunk = z - step if way == 0 else z + step
        got(pair_lags(chunk, core, sub), sring.at[way, step - 1, sub], rring.at[way, step - 1, sub])

    def pair_got(chunk_slot, chunk, sub):
        got(pair_lags(chunk, 1 - core, sub), spair.at[chunk_slot, sub], rpair.at[chunk_slot, sub])

    sent = []

    def go(desc):
        desc.start()
        sent.append(desc)

    for sub in range(2):
        for j in (2 * sub, 2 * sub + 1):
            got(wbuf.at[z * 8 + core * 4 + j], sb1.at[j], rb1.at[j])
        go(ring_send(0, 0, sub))
        go(ring_send(1, 0, sub))
        go(pair_send(0, z, sub))

    got(xraw.at[pl.ds(64 + 384 * 3, 384)], sa.at[3], ra.at[3])
    go(send(xraw.at[pl.ds(64 + 1536 - 64, 64)], xraw.at[pl.ds(0, 64)], sh.at[0], rh.at[0], ahead))
    for j in range(3):
        got(xraw.at[pl.ds(64 + 384 * j, 384)], sa.at[j], ra.at[j])
    got(xraw.at[pl.ds(0, 64)], sh.at[0], rh.at[0])
    xf[...] = xraw[...].astype(F32)
    first = jnp.logical_and(z == 0, core == 0)
    xf[0:64, :] = jnp.where(first, jnp.zeros((64, 128), F32), xf[0:64, :])
    xpf[:, 0:128] = xf[pl.ds(0, 800, stride=2), :]
    xpf[:, 128:256] = xf[pl.ds(1, 800, stride=2), :]
    for s in range(16):
        rows = 800 if s == 0 else 784
        xs[s, 0:rows, :] = xpf[pl.ds(s, rows), :].astype(BF)

    acc[...] = jnp.zeros_like(acc)

    def shifted(kappa):
        e = 32 - kappa
        s = lax.rem(e, 16)
        return xs[s, pl.ds(pl.multiple_of(e - s, 16), 768), :]

    def forward_chunk(zc):
        lag = zc * 8
        before = wbuf[lax.rem(lag + 63, 64)]
        before = jnp.where(zc == 0, jnp.zeros_like(before), before)
        left, right = [], []
        for d in range(4):
            low = wbuf[lag + 2 * d]
            prior = before if d == 0 else wbuf[lag + 2 * d - 1]
            high = wbuf[lag + 2 * d + 1]
            left.append(shifted(4 * zc + d))
            right.append(jnp.concatenate([jnp.concatenate([low, prior], 1), jnp.concatenate([high, low], 1)], 0))
        acc[...] += lax.dot_general(jnp.concatenate(left, 1), jnp.concatenate(right, 1), (((1,), (1,)), ((), ())),
                                    preferred_element_type=F32)

    for step in range(1, 5):
        for way, sub in ((0, 0), (1, 1), (0, 1), (1, 0)):
            if step == 4 and way != sub:
                continue
            ring_got(way, step, sub)
            if step < 3 or (step == 3 and way == sub):
                go(ring_send(way, step, sub))
            go(pair_send(2 * step - 1 + (way if step < 4 else 0), z - step if way == 0 else z + step, sub))
        if step == 1:
            for sub in range(2):
                pair_got(0, z, sub)
        for way, sub in ((0, 0), (1, 1), (0, 1), (1, 0)):
            if step == 4 and way != sub:
                continue
            pair_got(2 * step - 1 + (way if step < 4 else 0), z - step if way == 0 else z + step, sub)

        @pl.loop(0, 2)
        def _(i):
            forward_chunk(lax.rem(z + 8 + step - i * (2 * step - 1), 8))
    acc[:, 0:128] += lax.dot_general(xs[0, 0:768, 128:256], wbuf[63], (((1,), (1,)), ((), ())),
                                     preferred_element_type=F32)

    for k in (1, 2, 3):
        j = lax.rem(q + k, 4)
        csend[k - 1] = acc[pl.ds(pl.multiple_of(192 * j, 64), 192), :].astype(BF)
        go(send(csend.at[k - 1], crecv.at[3 - k], sc.at[k - 1], rc.at[3 - k], peer(j)))
    got(mraw, sm.at[0], rm.at[0])
    got(lraw, sm.at[1], rm.at[1])
    mf[...] = mraw[...].astype(F32)
    mine = pl.ds(pl.multiple_of(192 * q, 64), 192)
    total = acc[mine, :]
    for k in range(3):
        got(crecv.at[k], sc.at[k], rc.at[k])
        total = total + crecv[k].astype(F32)
    limit = lraw[0:1, :]
    for i in range(2):
        when = (2 * lax.broadcasted_iota(jnp.int32, (192, 128), 0) + i).astype(F32)
        gap = mf[pl.ds(i, 192, stride=2), :] - total[:, i * 128:(i + 1) * 128] * (1.0 / math.sqrt(LAGS * M))
        kept = jnp.where(when < limit, gap, 0.0).astype(BF)
        rall[mine, i * 128:(i + 1) * 128] = kept
        mf[pl.ds(i, 192, stride=2), :] = kept.astype(F32)
    for k in (1, 2, 3):
        go(send(rall.at[mine], rall.at[mine], sr.at[k - 1], rr.at[3 - k], peer(lax.rem(q + k, 4))))
    rout[...] = mf[...].astype(BF)
    start_any(rout, rres, sm.at[2], rm.at[2], t_in(q))
    for k in range(3):
        got(rall.at[pl.ds(pl.multiple_of(192 * lax.rem(q + k + 1, 4), 64), 192)], sr.at[k], rr.at[k])
    rt[...] = rall[...].astype(F32).T.astype(BF)

    def ring_add(step, way, sub):
        slot = 2 * step - (1 if way == 0 and step > 0 else 0)
        own = dall[slot, pl.ds(core * 4 + 2 * sub, 2)]
        own = own + dxr[slot, pl.ds(2 * sub, 2)].astype(F32)
        if step > (0 if way == sub else 1):
            got(gr.at[way, step - 1, sub], sg.at[way, step - 1, sub], rg.at[way, step - 1, sub])
            own = own + gr[way, step - 1, sub].astype(F32)
        gs[way, step, sub] = own.astype(BF)
        return send(gs.at[way, step, sub], gr.at[way, step, sub], sg.at[way, step, sub], rg.at[way, step, sub],
                    along(1 if way == 0 else -1))

    @pl.loop(0, 8)
    def _(pos):
        m = (pos + 1) // 2
        zc = lax.rem(z + 8 + (4 - m) * (2 * (pos % 2) - 1), 8)
        blocks = []
        for d in range(4):
            blocks.append(jnp.dot(rt[...], shifted(4 * zc + d), preferred_element_type=F32))
            if d > 0:
                dall[pos, 2 * d - 1] = blocks[d - 1][128:, :128] + blocks[d][:128, 128:]
            dall[pos, 2 * d] = blocks[d][:128, :128] + blocks[d][128:, 128:]
        last = jnp.dot(rt[0:128, :], shifted(4 * zc + 4)[:, 128:256], preferred_element_type=F32)
        dall[pos, 7] = blocks[3][128:, :128] + last
        dxs[pos] = dall[pos, pl.ds((1 - core) * 4, 4)].astype(BF)
        send(dxs.at[pos], dxr.at[pos], sdx.at[pos], rdx.at[pos], partner).start()
        for step in range(4):
            @pl.when(pos == 2 * step)
            def _():
                for slot in ((2 * step - 1, 2 * step) if step else (0,)):
                    got(dxr.at[slot], sdx.at[slot], rdx.at[slot])
                for way, sub in ((0, 0), (1, 1), (0, 1), (1, 0)):
                    if step or way == sub:
                        ring_add(step, way, sub).start()

    got(dxr.at[7], sdx.at[7], rdx.at[7])
    for sub in range(2):
        whole = dall[7, pl.ds(core * 4 + 2 * sub, 2)] + dxr[7, pl.ds(2 * sub, 2)].astype(F32)
        for way in range(2):
            got(gr.at[way, 3, sub], sg.at[way, 3, sub], rg.at[way, 3, sub])
            whole = whole + gr[way, 3, sub].astype(F32)
        fs[pl.ds(2 * sub, 2)] = whole.astype(BF)
        for j in (2 * sub, 2 * sub + 1):
            start_any(fs.at[j], fr.at[q], sf.at[j], rf.at[q], t_in(j))

    got(rres, sm.at[2], rm.at[2])
    res_ref[...] = rres[...]
    for c in range(4):
        got(fr.at[c], sf.at[c], rf.at[c])
        cols = slice(c * 128, (c + 1) * 128)
        new_ref[:, cols] = par_ref[:, cols] + fr[c].astype(F32) * (0.5 / math.sqrt(24576))

    for desc in sent:
        desc.wait_send()
    for c in range(4):
        done_any(wsend.at[c], wbuf.at[tm], sb1.at[c], rb1.at[x], t_out(c))
        done_any(rec_ref, xraw.at[own_rows], sa.at[c], ra.at[x], spread(c))
        done_any(fs.at[c], fr.at[q], sf.at[c], rf.at[q], t_in(c))
    done_any(meas_ref, mraw, sm.at[0], rm.at[0], t_out(x))
    done_any(lsend, lraw, sm.at[1], rm.at[1], t_out(x))
    done_any(rout, rres, sm.at[2], rm.at[2], t_in(q))

    @pl.loop(0, 8)
    def _(pos):
        send(dxs.at[pos], dxr.at[pos], sdx.at[pos], rdx.at[pos], partner).wait_send()
    for step in range(4):
        for way in range(2):
            for sub in range(2):
                if step or way == sub:
                    send(gs.at[way, step, sub], gr.at[way, step, sub], sg.at[way, step, sub], rg.at[way, step, sub],
                         along(1 if way == 0 else -1)).wait_send()


def on_device(records, measured, markov_params, seg_lengths):
    dma = pltpu.SemaphoreType.DMA
    new, res = pl.pallas_call(
        body,
        out_shape=(jax.ShapeDtypeStruct((128, 512), F32), jax.ShapeDtypeStruct((384, 128), BF)),
        in_specs=[pl.BlockSpec(memory_space=pltpu.SMEM)] + [pl.BlockSpec(memory_space=pltpu.VMEM)] * 3,
        out_specs=(pl.BlockSpec(memory_space=pltpu.VMEM), pl.BlockSpec(memory_space=pltpu.VMEM)),
        scratch_shapes=[
            pltpu.VMEM((4, 128, 128), BF),
            pltpu.VMEM((64, 128, 128), BF),
            pltpu.VMEM((1600, 128), BF),
            pltpu.VMEM((1600, 128), F32),
            pltpu.VMEM((800, 256), F32),
            pltpu.VMEM((16, 800, 256), BF),
            pltpu.VMEM((8, 128), F32),
            pltpu.VMEM((8, 128), F32),
            pltpu.VMEM((384, 128), BF),
            pltpu.VMEM((384, 128), F32),
            pltpu.VMEM((768, 256), F32),
            pltpu.VMEM((3, 192, 256), BF),
            pltpu.VMEM((3, 192, 256), BF),
            pltpu.VMEM((768, 256), BF),
            pltpu.VMEM((256, 768), BF),
            pltpu.VMEM((384, 128), BF),
            pltpu.VMEM((384, 128), BF),
            pltpu.VMEM((8, 8, 128, 128), F32),
            pltpu.VMEM((8, 4, 128, 128), BF),
            pltpu.VMEM((8, 4, 128, 128), BF),
            pltpu.VMEM((2, 4, 2, 2, 128, 128), BF),
            pltpu.VMEM((2, 4, 2, 2, 128, 128), BF),
            pltpu.VMEM((4, 128, 128), BF),
            pltpu.VMEM((4, 128, 128), BF),
            dma((4,)), dma((4,)), dma((4,)), dma((4,)), dma((3,)), dma((3,)), dma((1,)), dma((1,)),
            dma((2, 4, 2)), dma((2, 4, 2)), dma((8, 2)), dma((8, 2)), dma((3,)), dma((3,)), dma((3,)), dma((3,)),
            dma((8,)), dma((8,)), dma((2, 4, 2)), dma((2, 4, 2)), dma((4,)), dma((4,)),
        ],
        compiler_params=pltpu.CompilerParams(collective_id=0, has_side_effects=True, vmem_limit_bytes=56 * 1024 * 1024),
        name="gradient_step",
    )(seg_lengths, records, measured, markov_params.reshape(128, 512))
    return new.reshape(1, 128, 512), res


def solution(mesh):
    in_specs = (P("tm", "grp"), P("tm", "grp"), P("tm", "grp", None), P("tm"))
    out_specs = (P("tm", "grp", None), P("tm", "grp"))
    return jax.shard_map(on_device, mesh=mesh, in_specs=in_specs, out_specs=out_specs, check_vma=False)
```

time: 971 us -> 81.9 us (0.08)
  the two profiles are of different devices: /device:TPU:8 before, /device:TPU:1 now
where the time goes in v1:
time: 81.9 us; the launch traced here: 80.3 us
  Pallas kernels  76.6 us (94%)
  local copies, waits for them, and re-layouts  2.35 us (3%)
  between operations  1.29 us (2%)
    pallas_call x1, Pallas kernels, on_device(): pl.pallas_call(body, out_shape=(jax.ShapeDtypeStruct((128, 512), F32), ja...  76.6 us
    unnamed x4, local copies, waits for them, and re-layouts  2.35 us

profile of v1, /device:TPU:1, one launch (start us, length us, event | category | flops | bytes accessed | tf_op | source)
XLA Modules:
  0.0 80.3 jit_solution(10699814823713746367)
XLA Ops:
  1.3 76.6 %gradient_step.1 = (f32[128,512]{1,0:T(8,128)}, bf16[384,128]{1,0:T(8,128)(2,1)}) custom-call(s32[1]{0:T(128)S(6)} %copy.8.len_ref, bf16[384,128]{1,0:T(8,128)(2,1)} %rec_ref.1, bf16[384,128]{1,0:T(8,128)(2,1)} %meas_ref.1, f32[128,512]{1,0:T(8,128)} %bitcast.2), custom_call_target="tpu_custom_call" | custom-call | tf_op jit(solution)/shard_map/gradient_step/pallas_call | solution.py:292
  77.9 0.0 copy-start
  77.9 1.7 %copy.9 = f32[1,128,512]{2,1,0:T(8,128)} copy(f32[1,128,512]{2,1,0:T(8,128)} %bitcast.3) | data formatting | bytes 524288
  79.6 0.0 copy-done
  79.6 0.6 copy.10
Async XLA Ops:
  77.9 1.7 %copy-start = (bf16[384,128]{1,0:T(8,128)(2,1)S(1)}, bf16[384,128]{1,0:T(8,128)(2,1)}, u32[]{:S(2)}) copy-start(bf16[384,128]{1,0:T(8,128)(2,1)} %get-tuple-element.9) | copy-start | bytes 294916

commit v2 on v0

v2 whole, which is shorter than its diff:
```python
import math

import jax
import jax.numpy as jnp
from jax import lax
from jax.experimental import pallas as pl
from jax.experimental.pallas import tpu as pltpu
from jax.sharding import PartitionSpec as P

M = 512
LAGS = 64
BF = jnp.bfloat16
F32 = jnp.float32
HALO = 128
SPAN = 1536


def body(len_ref, rec_ref, meas_ref, par_ref, new_ref, res_ref, wsend, wbuf, xbuf, xt, msend, mrecv, mtf, mtime, lsend,
         lraw, acc, cbuf, ubuf, rp, wq, qq, qs, rsend, rrecv, dall, dxs, dxr, gs, gr, fs, fr,
         sb1, rb1, sa, sa2, sb2, ra, sm, rm, sl, rl, so, ro, sh, rh, sring, rring, spair, rpair, sdx, rdx, sg, rg, sf, rf):
    tm = lax.axis_index("tm")
    grp = lax.axis_index("grp")
    z = tm // 8
    yh = (tm // 4) % 2
    x = tm % 4
    yl = grp // 2
    core = grp % 2
    q = yl * 2 + yh
    home = yh == core

    def spread(j):
        return z * 8 + core * 4 + j, yl * 2 + yh

    def along(step):
        return lax.rem(z + step + 8, 8) * 8 + yh * 4 + x, grp

    def over_x(k):
        return z * 8 + yh * 4 + lax.rem(x + k, 4), grp

    def over_y(k):
        j = lax.rem(q + k, 4)
        return z * 8 + (j % 2) * 4 + x, (j // 2) * 2 + core

    partner = (tm, yl * 2 + 1 - core)
    ahead = (lax.rem(z + core, 8) * 8 + yh * 4 + x, yl * 2 + 1 - core)
    behind = (lax.rem(z + core + 7, 8) * 8 + yh * 4 + x, yl * 2 + 1 - core)

    def first_hop(j):
        xj = core * x + (1 - core) * j
        yhj = core * (j % 2) + (1 - core) * yh
        ylj = core * (j // 2) + (1 - core) * yl
        return z * 8 + yhj * 4 + xj, ylj * 2 + yh

    def hop_from(j, c):
        if c == 0:
            return z * 8 + yh * 4 + j, yl * 2
        return z * 8 + core * 4 + x, j * 2 + 1

    def is_me(dev):
        return jnp.logical_and(dev[0] == tm, dev[1] == grp)

    def where(dev):
        return dict(device_id={"tm": dev[0], "grp": dev[1]}, device_id_type=pl.DeviceIdType.MESH)

    def send(src, dst, ssem, rsem, dev):
        return pltpu.make_async_remote_copy(src_ref=src, dst_ref=dst, send_sem=ssem, recv_sem=rsem, **where(dev))

    sent = []

    def go(src, dst, ssem, rsem, dev, only=None):
        desc = send(src, dst, ssem, rsem, dev)
        if only is None:
            desc.start()
            sent.append(desc.wait_send)
            return

        @pl.when(only)
        def _():
            desc.start()

        def wait():
            @pl.when(only)
            def _():
                send(src, dst, ssem, rsem, dev).wait_send()
        sent.append(wait)

    def go_any(src, dst, ssem, rsem, dev):
        me = is_me(dev)

        @pl.when(me)
        def _():
            pltpu.make_async_copy(src, dst, rsem).start()
        go(src, dst, ssem, rsem, dev, jnp.logical_not(me))

    def got(dst, ssem, rsem):
        send(dst, dst, ssem, rsem, partner).wait_recv()

    barrier = pltpu.get_barrier_semaphore()
    count = jnp.int32(0)
    friends = [(spread(j), True) for j in range(4)] + [(first_hop(j), True) for j in range(4)]
    friends += [(hop_from(j, 0), home) for j in range(4)] + [(hop_from(j, 1), True) for j in range(2)]
    for n, (dev, holds) in enumerate(friends):
        other = jnp.logical_and(jnp.logical_not(is_me(dev)), holds)
        count = count + other.astype(jnp.int32)

        @pl.when(other)
        def _():
            pl.semaphore_signal(barrier, inc=1, **where(dev))
    sure = [over_x(k) for k in (1, 2, 3)] + [over_y(k) for k in (1, 2, 3)]
    sure += [along(1), along(-1), partner, ahead, behind]
    for dev in sure:
        pl.semaphore_signal(barrier, inc=1, **where(dev))
    wsend[...] = par_ref[...].astype(BF)
    lsend[...] = jnp.full((8, 128), len_ref[0], jnp.int32).astype(F32)
    msend[...] = meas_ref[...].astype(F32).T.astype(BF)
    xbuf[0:64, :] = jnp.zeros((64, 512), BF)
    mtf[32:128, :] = jnp.zeros((96, SPAN), F32)
    rp[...] = jnp.zeros_like(rp)
    acc[...] = jnp.zeros_like(acc)
    pl.semaphore_wait(barrier, count + len(sure))

    def lag_rows(chunk, half, sub):
        return wbuf.at[pl.ds(pl.multiple_of(lax.rem(chunk + 8, 8) * 256 + half * 128 + sub * 32, 32), 32)]

    def slot(g, j):
        return xbuf.at[pl.ds(pl.multiple_of(HALO + 384 * j, 128), 384), pl.ds(pl.multiple_of(128 * g, 128), 128)]

    for j in range(4):
        go_any(wsend.at[pl.ds(32 * j, 32)], lag_rows(z, yh, x), sb1.at[j], rb1.at[x], spread(j))
    for j in range(4):
        go_any(rec_ref, slot(grp, x), sa.at[j], ra.at[grp * 4 + x], first_hop(j))

    def ring_send(way, step, sub):
        ref = lag_rows(z - step if way == 0 else z + step, core, sub)
        go(ref, ref, sring.at[way, step, sub], rring.at[way, step, sub], along(1 if way == 0 else -1))

    def ring_got(way, step, sub):
        ref = lag_rows(z - step if way == 0 else z + step, core, sub)
        got(ref, sring.at[way, step - 1, sub], rring.at[way, step - 1, sub])

    def pair_send(n, chunk, sub):
        ref = lag_rows(chunk, core, sub)
        go(ref, ref, spair.at[n, sub], rpair.at[n, sub], partner)

    def pair_got(n, chunk, sub):
        got(lag_rows(chunk, 1 - core, sub), spair.at[n, sub], rpair.at[n, sub])

    def number(way, step):
        return 2 * step - 1 + (way if step < 4 else 0)

    for sub in range(4):
        got(lag_rows(z, core, sub), sb1.at[sub], rb1.at[sub])
        ring_send(0, 0, sub)
        ring_send(1, 0, sub)
        pair_send(0, z, sub)

    def slot_got(g, j):
        got(slot(g, j), sa.at[0], ra.at[g * 4 + j])

    def turned(g, j):
        cols = pl.ds(pl.multiple_of(HALO + 384 * j, 128), 384)
        rows = pl.ds(pl.multiple_of(128 * g, 128), 128)
        xt[rows, cols] = xbuf[cols, rows].T

    for n in range(2):
        g = 2 * n + 1
        slot_got(g, x)
        for k in (1, 2, 3):
            go(slot(g, x), slot(g, x), sb2.at[n, k - 1], ra.at[g * 4 + x], over_x(k))
    for j in range(4):
        @pl.when(home)
        def _():
            slot_got(yl * 2, j)
        for k in (1, 2, 3):
            go(slot(yl * 2, j), slot(yl * 2, j), sa2.at[j, k - 1], ra.at[yl * 8 + j], over_y(k), home)
    for j in range(4):
        go_any(msend.at[pl.ds(32 * j, 32)], mrecv.at[x], sm.at[j], rm.at[x], spread(j))
        go_any(lsend, lraw.at[x], sl.at[j], rl.at[x], spread(j))

    ways = ((0, (0, 1)), (1, (2, 3)), (0, (2, 3)), (1, (0, 1)))
    for step in range(1, 5):
        for n, (way, subs) in enumerate(ways):
            if step == 4 and n >= 2:
                continue
            for sub in subs:
                ring_got(way, step, sub)
                if step < 3 or (step == 3 and n < 2):
                    ring_send(way, step, sub)
                pair_send(number(way, step), z - step if way == 0 else z + step, sub)
        if step == 2:
            for j in range(4):
                got(mrecv.at[j], sm.at[j], rm.at[j])
                got(lraw.at[j], sl.at[j], rl.at[j])
                mtf[0:32, 384 * j:384 * (j + 1)] = mrecv[j].astype(F32)
            mtime[...] = mtf[...].T
            for n in range(2):
                turned(2 * n + 1, x)
            for j in range(4):
                @pl.when(jnp.logical_not(home))
                def _():
                    slot_got(yl * 2, j)
                turned(yl * 2, j)
        if step == 3:
            for j in range(4):
                g = 2 * (1 - yl)
                slot_got(g, j)
                turned(g, j)
    for k in (1, 3, 2):
        for n in range(2):
            j = lax.rem(x + k, 4)
            slot_got(2 * n + 1, j)
            turned(2 * n + 1, j)
    last_rows = xbuf.at[pl.ds(HALO + SPAN - 64, 64)]
    halo_rows = xbuf.at[pl.ds(HALO - 64, 64)]
    go(last_rows, halo_rows, sh.at[0], rh.at[0], ahead)
    for sub in range(4):
        pair_got(0, z, sub)
    for step in range(1, 5):
        for n, (way, subs) in enumerate(ways):
            if step == 4 and n >= 2:
                continue
            for sub in subs:
                pair_got(number(way, step), z - step if way == 0 else z + step, sub)
    got(halo_rows, sh.at[0], rh.at[0])
    first = jnp.logical_and(z == 0, core == 0)
    halo = xbuf[HALO - 64:HALO, :]
    halo = jnp.where(first, jnp.zeros_like(halo), halo)
    xbuf[HALO - 64:HALO, :] = halo
    xt[:, 0:HALO] = xbuf[0:HALO, :].T

    @pl.loop(0, 8)
    def _(c):
        w = wbuf[pl.ds(pl.multiple_of(c * 256, 256), 256), :]

        @pl.loop(0, 4)
        def _(i):
            part = lax.dot_general(xbuf[pl.ds(pl.multiple_of(64 + 400 * i, 16), 400), :], w, (((1,), (1,)), ((), ())),
                                   preferred_element_type=F32)
            acc[pl.ds(pl.multiple_of(400 * i + 8 * c, 8), 400), :] += part

    cbuf[...] = acc[48:1600, 0:128] + acc[44:1596, 128:256]
    ubuf[...] = cbuf[8:1552, :] + pltpu.roll(cbuf[6:1550, :], 64, 1)
    lane = lax.broadcasted_iota(jnp.int32, (384, 128), 1)
    row = lax.broadcasted_iota(jnp.int32, (384, 128), 0).astype(F32)
    for j in range(4):
        lo = 384 * j
        total = ubuf[lo + 8:lo + 392, :] + pltpu.roll(ubuf[lo + 7:lo + 391, :], 96, 1)
        gap = mtime[lo:lo + 384, :] - total * (1.0 / math.sqrt(LAGS * M))
        keep = jnp.logical_and(row < lraw[j, 0:1, :], lane < 32)
        rp[HALO + lo:HALO + lo + 384, :] = jnp.where(keep, gap, 0.0).astype(BF).astype(F32)
    wq[...] = rp[0:1736, :] + pltpu.roll(rp[1:1737, :], 32, 1)
    qq[...] = wq[0:1732, :] + pltpu.roll(wq[2:1734, :], 64, 1)
    for n in range(2):
        qs[n, :, 0:128] = qq[8 * n:8 * n + 1712, :].astype(BF)
        qs[n, :, 128:256] = qq[8 * n + 4:8 * n + 1716, :].astype(BF)

    def ring_add(step, way, sub):
        at = 2 * step - (1 if way == 0 and step > 0 else 0)
        rows = pl.ds(128 * sub, 128)
        own = dall[at, core, rows, :] + dxr[at, rows, :].astype(F32)
        early = (sub < 2) == (way == 0)
        if step > (0 if early else 1):
            got(gr.at[way, step - 1, sub], sg.at[way, step - 1, sub], rg.at[way, step - 1, sub])
            own = own + gr[way, step - 1, sub].astype(F32)
        gs[way, step, sub] = own.astype(BF)
        return send(gs.at[way, step, sub], gr.at[way, step, sub], sg.at[way, step, sub], rg.at[way, step, sub],
                    along(1 if way == 0 else -1))

    @pl.loop(0, 8)
    def _(pos):
        m = (pos + 1) // 2
        zc = lax.rem(z + 8 + (4 - m) * (2 * (pos % 2) - 1), 8)
        odd = zc % 2
        part = jnp.dot(xt[...], qs[odd, pl.ds(pl.multiple_of(8 * (zc - odd), 16), HALO + SPAN), :],
                       preferred_element_type=F32)
        dall[pos, 0] = part[:, 0:128]
        dall[pos, 1] = part[:, 128:256]
        dxs[pos] = dall[pos, 1 - core].astype(BF)
        send(dxs.at[pos], dxr.at[pos], sdx.at[pos], rdx.at[pos], partner).start()
        for step in range(4):
            @pl.when(pos == 2 * step)
            def _():
                for at in ((2 * step - 1, 2 * step) if step else (0,)):
                    got(dxr.at[at], sdx.at[at], rdx.at[at])
                for n, (way, subs) in enumerate(ways):
                    if step or n < 2:
                        for sub in subs:
                            ring_add(step, way, sub).start()

    back = rp[HALO:HALO + SPAN, :].T
    for j in range(4):
        rsend[j] = back[0:32, 384 * j:384 * (j + 1)].astype(BF)
        go_any(rsend.at[j], rrecv.at[pl.ds(pl.multiple_of(32 * x, 32), 32)], so.at[j], ro.at[x], spread(j))
    for j in range(4):
        got(rrecv.at[pl.ds(32 * j, 32)], so.at[j], ro.at[j])
    res_ref[...] = rrecv[...].astype(F32).T.astype(BF)

    got(dxr.at[7], sdx.at[7], rdx.at[7])
    for sub in range(4):
        rows = pl.ds(128 * sub, 128)
        whole = dall[7, core, rows, :] + dxr[7, rows, :].astype(F32)
        for way in range(2):
            got(gr.at[way, 3, sub], sg.at[way, 3, sub], rg.at[way, 3, sub])
            whole = whole + gr[way, 3, sub].astype(F32)
        fs[:, 128 * sub:128 * (sub + 1)] = whole.T.astype(BF)
    for j in range(4):
        go_any(fs.at[pl.ds(32 * j, 32)], fr.at[pl.ds(pl.multiple_of(32 * x, 32), 32)], sf.at[j], rf.at[x], spread(j))
    for j in range(4):
        rows = pl.ds(32 * j, 32)
        got(fr.at[rows], sf.at[j], rf.at[j])
        new_ref[rows, :] = par_ref[rows, :] + fr[rows, :].astype(F32) * (0.5 / math.sqrt(24576))

    for wait in sent:
        wait()

    @pl.loop(0, 8)
    def _(pos):
        send(dxs.at[pos], dxr.at[pos], sdx.at[pos], rdx.at[pos], partner).wait_send()
    for step in range(4):
        for n, (way, subs) in enumerate(ways):
            if step or n < 2:
                for sub in subs:
                    send(gs.at[way, step, sub], gr.at[way, step, sub], sg.at[way, step, sub], rg.at[way, step, sub],
                         along(1 if way == 0 else -1)).wait_send()


def on_device(records, measured, markov_params, seg_lengths):
    dma = pltpu.SemaphoreType.DMA
    new, res = pl.pallas_call(
        body,
        out_shape=(jax.ShapeDtypeStruct((128, 512), F32), jax.ShapeDtypeStruct((384, 128), BF)),
        in_specs=[pl.BlockSpec(memory_space=pltpu.SMEM)] + [pl.BlockSpec(memory_space=pltpu.VMEM)] * 3,
        out_specs=(pl.BlockSpec(memory_space=pltpu.VMEM), pl.BlockSpec(memory_space=pltpu.VMEM)),
        scratch_shapes=[
            pltpu.VMEM((128, 512), BF),
            pltpu.VMEM((2048, 512), BF),
            pltpu.VMEM((HALO + SPAN, 512), BF),
            pltpu.VMEM((512, HALO + SPAN), BF),
            pltpu.VMEM((128, 384), BF),
            pltpu.VMEM((4, 32, 384), BF),
            pltpu.VMEM((128, SPAN), F32),
            pltpu.VMEM((SPAN, 128), F32),
            pltpu.VMEM((8, 128), F32),
            pltpu.VMEM((4, 8, 128), F32),
            pltpu.VMEM((1664, 256), F32),
            pltpu.VMEM((1552, 128), F32),
            pltpu.VMEM((1544, 128), F32),
            pltpu.VMEM((1744, 128), F32),
            pltpu.VMEM((1736, 128), F32),
            pltpu.VMEM((1732, 128), F32),
            pltpu.VMEM((2, 1712, 256), BF),
            pltpu.VMEM((4, 32, 384), BF),
            pltpu.VMEM((128, 384), BF),
            pltpu.VMEM((8, 2, 512, 128), F32),
            pltpu.VMEM((8, 512, 128), BF),
            pltpu.VMEM((8, 512, 128), BF),
            pltpu.VMEM((2, 4, 4, 128, 128), BF),
            pltpu.VMEM((2, 4, 4, 128, 128), BF),
            pltpu.VMEM((128, 512), BF),
            pltpu.VMEM((128, 512), BF),
            dma((4,)), dma((4,)), dma((4,)), dma((4, 3)), dma((2, 3)), dma((16,)), dma((4,)), dma((4,)), dma((4,)), dma((4,)),
            dma((4,)), dma((4,)), dma((1,)), dma((1,)),
            dma((2, 4, 4)), dma((2, 4, 4)), dma((8, 4)), dma((8, 4)),
            dma((8,)), dma((8,)), dma((2, 4, 4)), dma((2, 4, 4)), dma((4,)), dma((4,)),
        ],
        compiler_params=pltpu.CompilerParams(collective_id=0, has_side_effects=True, vmem_limit_bytes=56 * 1024 * 1024),
        name="gradient_step",
    )(seg_lengths, records, measured, markov_params.reshape(128, 512))
    return new.reshape(1, 128, 512), res


def solution(mesh):
    in_specs = (P("tm", "grp"), P("tm", "grp"), P("tm", "grp", None), P("tm"))
    out_specs = (P("tm", "grp", None), P("tm", "grp"))
    return jax.shard_map(on_device, mesh=mesh, in_specs=in_specs, out_specs=out_specs, check_vma=False)
```

time: 971 us -> 75.8 us (0.08)
  the two profiles are of different devices: /device:TPU:8 before, /device:TPU:1 now
where the time goes in v2:
time: 75.8 us; the launch traced here: 75.7 us
  Pallas kernels  72.1 us (95%)
  local copies, waits for them, and re-layouts  2.35 us (3%)
  between operations  1.29 us (2%)
    pallas_call x1, Pallas kernels, on_device(): pl.pallas_call(body, out_shape=(jax.ShapeDtypeStruct((128, 512), F32), ja...  72.1 us
    unnamed x4, local copies, waits for them, and re-layouts  2.35 us

profile of v2, /device:TPU:1, one launch (start us, length us, event | category | flops | bytes accessed | tf_op | source)
XLA Modules:
  0.0 75.7 jit_solution(10112727316808137390)
XLA Ops:
  1.3 72.1 %gradient_step.1 = (f32[128,512]{1,0:T(8,128)}, bf16[384,128]{1,0:T(8,128)(2,1)}) custom-call(s32[1]{0:T(128)S(6)} %copy.8.len_ref, bf16[384,128]{1,0:T(8,128)(2,1)} %rec_ref.1, bf16[384,128]{1,0:T(8,128)(2,1)} %meas_ref.1, f32[128,512]{1,0:T(8,128)} %bitcast.2), custom_call_target="tpu_custom_call" | custom-call | tf_op jit(solution)/shard_map/gradient_step/pallas_call | solution.py:329
  73.3 0.0 copy-start
  73.3 1.7 %copy.9 = f32[1,128,512]{2,1,0:T(8,128)} copy(f32[1,128,512]{2,1,0:T(8,128)} %bitcast.3) | data formatting | bytes 524288
  75.1 0.0 copy-done
  75.1 0.6 copy.10
Async XLA Ops:
  73.3 1.7 %copy-start = (bf16[384,128]{1,0:T(8,128)(2,1)S(1)}, bf16[384,128]{1,0:T(8,128)(2,1)}, u32[]{:S(2)}) copy-start(bf16[384,128]{1,0:T(8,128)(2,1)} %get-tuple-element.9) | copy-start | bytes 294916

commit v3 on v2

--- a/solution.py
+++ b/solution.py
@@ -28,8 +28,8 @@
     q = yl * 2 + yh
     home = yh == core
 
-    def spread(j):
-        return z * 8 + core * 4 + j, yl * 2 + yh
+    def spread(j, dz=0):
+        return lax.rem(z + dz + 8, 8) * 8 + core * 4 + j, yl * 2 + yh
 
     def along(step):
         return lax.rem(z + step + 8, 8) * 8 + yh * 4 + x, grp
@@ -68,15 +68,14 @@
     sent = []
 
     def go(src, dst, ssem, rsem, dev, only=None):
-        desc = send(src, dst, ssem, rsem, dev)
         if only is None:
-            desc.start()
-            sent.append(desc.wait_send)
+            send(src, dst, ssem, rsem, dev).start()
+            sent.append(lambda: send(src, dst, ssem, rsem, dev).wait_send())
             return
 
         @pl.when(only)
         def _():
-            desc.start()
+            send(src, dst, ssem, rsem, dev).start()
 
         def wait():
             @pl.when(only)
@@ -97,7 +96,7 @@
 
     barrier = pltpu.get_barrier_semaphore()
     count = jnp.int32(0)
-    friends = [(spread(j), True) for j in range(4)] + [(first_hop(j), True) for j in range(4)]
+    friends = [(spread(j, dz), True) for dz in (1, -1) for j in range(4)] + [(spread(j), True) for j in range(4)] + [(first_hop(j), True) for j in range(4)]
     friends += [(hop_from(j, 0), home) for j in range(4)] + [(hop_from(j, 1), True) for j in range(2)]
     for n, (dev, holds) in enumerate(friends):
         other = jnp.logical_and(jnp.logical_not(is_me(dev)), holds)
@@ -112,23 +111,27 @@
         pl.semaphore_signal(barrier, inc=1, **where(dev))
     wsend[...] = par_ref[...].astype(BF)
     lsend[...] = jnp.full((8, 128), len_ref[0], jnp.int32).astype(F32)
+    pl.semaphore_wait(barrier, count + len(sure))
+
+    def lag_rows(chunk, half, sub):
+        return wbuf.at[pl.ds(pl.multiple_of(lax.rem(chunk + 8, 8) * 256 + half * 128 + sub * 32, 32), 32)]
+
+    def slot(g, j):
+        return xbuf.at[pl.ds(pl.multiple_of(HALO + 384 * j, 128), 384), pl.ds(pl.multiple_of(128 * g, 128), 128)]
+
+    for j in range(4):
+        go_any(wsend.at[pl.ds(32 * j, 32)], lag_rows(z, yh, x), sb1.at[j], rb1.at[x], spread(j))
+    for j in range(4):
+        go_any(rec_ref, slot(grp, x), sa.at[j], ra.at[grp * 4 + x], first_hop(j))
+
     msend[...] = meas_ref[...].astype(F32).T.astype(BF)
+    for j in range(4):
+        go_any(msend.at[pl.ds(32 * j, 32)], mrecv.at[x], sm.at[j], rm.at[x], spread(j))
+        go_any(lsend, lraw.at[x], sl.at[j], rl.at[x], spread(j))
     xbuf[0:64, :] = jnp.zeros((64, 512), BF)
     mtf[32:128, :] = jnp.zeros((96, SPAN), F32)
     rp[...] = jnp.zeros_like(rp)
     acc[...] = jnp.zeros_like(acc)
-    pl.semaphore_wait(barrier, count + len(sure))
-
-    def lag_rows(chunk, half, sub):
-        return wbuf.at[pl.ds(pl.multiple_of(lax.rem(chunk + 8, 8) * 256 + half * 128 + sub * 32, 32), 32)]
-
-    def slot(g, j):
-        return xbuf.at[pl.ds(pl.multiple_of(HALO + 384 * j, 128), 384), pl.ds(pl.multiple_of(128 * g, 128), 128)]
-
-    for j in range(4):
-        go_any(wsend.at[pl.ds(32 * j, 32)], lag_rows(z, yh, x), sb1.at[j], rb1.at[x], spread(j))
-    for j in range(4):
-        go_any(rec_ref, slot(grp, x), sa.at[j], ra.at[grp * 4 + x], first_hop(j))
 
     def ring_send(way, step, sub):
         ref = lag_rows(z - step if way == 0 else z + step, core, sub)
@@ -138,21 +141,26 @@
         ref = lag_rows(z - step if way == 0 else z + step, core, sub)
         got(ref, sring.at[way, step - 1, sub], rring.at[way, step - 1, sub])
 
-    def pair_send(n, chunk, sub):
-        ref = lag_rows(chunk, core, sub)
-        go(ref, ref, spair.at[n, sub], rpair.at[n, sub], partner)
+    def pair_copy(way, step, sub):
+        ref = lag_rows(z - step if way == 0 else z + step, core, sub)
+        n = number(way, step)
+        return send(ref, ref, spair.at[n, sub], rpair.at[n, sub], partner)
+
+    def pair_send(way, step, sub):
+        pair_copy(way, step, sub).start()
+        sent.append(lambda: pair_copy(way, step, sub).wait_send())
 
     def pair_got(n, chunk, sub):
         got(lag_rows(chunk, 1 - core, sub), spair.at[n, sub], rpair.at[n, sub])
 
     def number(way, step):
-        return 2 * step - 1 + (way if step < 4 else 0)
+        return 2 * step - 1 + (way if step < 4 else 0) if step else 0
 
     for sub in range(4):
         got(lag_rows(z, core, sub), sb1.at[sub], rb1.at[sub])
         ring_send(0, 0, sub)
         ring_send(1, 0, sub)
-        pair_send(0, z, sub)
+        pair_send(0, 0, sub)
 
     def slot_got(g, j):
         got(slot(g, j), sa.at[0], ra.at[g * 4 + j])
@@ -167,18 +175,29 @@
         slot_got(g, x)
         for k in (1, 2, 3):
             go(slot(g, x), slot(g, x), sb2.at[n, k - 1], ra.at[g * 4 + x], over_x(k))
-    for j in range(4):
+    for n in range(4):
+        j = lax.rem(x + 4 - n, 4)
+
         @pl.when(home)
         def _():
             slot_got(yl * 2, j)
         for k in (1, 2, 3):
-            go(slot(yl * 2, j), slot(yl * 2, j), sa2.at[j, k - 1], ra.at[yl * 8 + j], over_y(k), home)
-    for j in range(4):
-        go_any(msend.at[pl.ds(32 * j, 32)], mrecv.at[x], sm.at[j], rm.at[x], spread(j))
-        go_any(lsend, lraw.at[x], sl.at[j], rl.at[x], spread(j))
+            go(slot(yl * 2, j), slot(yl * 2, j), sa2.at[n, k - 1], ra.at[yl * 8 + j], over_y(k), home)
+
+    def arrived(n):
+        j = lax.rem(x + 4 - n, 4)
+
+        @pl.when(jnp.logical_not(home))
+        def _():
+            slot_got(yl * 2, j)
+        slot_got(2 * (1 - yl), j)
+        for g in range(4):
+            if n and g % 2:
+                slot_got(g, j)
+            turned(g, j)
 
     ways = ((0, (0, 1)), (1, (2, 3)), (0, (2, 3)), (1, (0, 1)))
-    for step in range(1, 5):
+    def passed_on(step):
         for n, (way, subs) in enumerate(ways):
             if step == 4 and n >= 2:
                 continue
@@ -186,41 +205,48 @@
                 ring_got(way, step, sub)
                 if step < 3 or (step == 3 and n < 2):
                     ring_send(way, step, sub)
-                pair_send(number(way, step), z - step if way == 0 else z + step, sub)
-        if step == 2:
-            for j in range(4):
-                got(mrecv.at[j], sm.at[j], rm.at[j])
-                got(lraw.at[j], sl.at[j], rl.at[j])
-                mtf[0:32, 384 * j:384 * (j + 1)] = mrecv[j].astype(F32)
-            mtime[...] = mtf[...].T
-            for n in range(2):
-                turned(2 * n + 1, x)
-            for j in range(4):
-                @pl.when(jnp.logical_not(home))
-                def _():
-                    slot_got(yl * 2, j)
-                turned(yl * 2, j)
-        if step == 3:
-            for j in range(4):
-                g = 2 * (1 - yl)
-                slot_got(g, j)
-                turned(g, j)
-    for k in (1, 3, 2):
-        for n in range(2):
-            j = lax.rem(x + k, 4)
-            slot_got(2 * n + 1, j)
-            turned(2 * n + 1, j)
-    last_rows = xbuf.at[pl.ds(HALO + SPAN - 64, 64)]
-    halo_rows = xbuf.at[pl.ds(HALO - 64, 64)]
-    go(last_rows, halo_rows, sh.at[0], rh.at[0], ahead)
-    for sub in range(4):
-        pair_got(0, z, sub)
-    for step in range(1, 5):
+                pair_send(way, step, sub)
+
+    def paired(step):
         for n, (way, subs) in enumerate(ways):
             if step == 4 and n >= 2:
                 continue
             for sub in subs:
                 pair_got(number(way, step), z - step if way == 0 else z + step, sub)
+
+    halo_rows = xbuf.at[pl.ds(HALO - 64, 64)]
+    last_rows = xbuf.at[pl.ds(HALO + SPAN - 64, 64)]
+
+    def forward(c, lo, rows):
+        part = lax.dot_general(xbuf[lo:lo + rows, :], wbuf[pl.ds(pl.multiple_of(c * 256, 256), 256), :],
+                               (((1,), (1,)), ((), ())), preferred_element_type=F32)
+        acc[pl.ds(pl.multiple_of(lo - 64 + 8 * c, 8), rows), :] += part
+
+    for step in range(1, 4):
+        passed_on(step)
+    for j in range(4):
+        got(mrecv.at[j], sm.at[j], rm.at[j])
+        got(lraw.at[j], sl.at[j], rl.at[j])
+        mtf[0:32, 384 * j:384 * (j + 1)] = mrecv[j].astype(F32)
+    mtime[...] = mtf[...].T
+    for n in range(4):
+        arrived(n)
+    go(last_rows, halo_rows, sh.at[0], rh.at[0], ahead)
+    for sub in range(4):
+        pair_got(0, z, sub)
+    for step in range(1, 4):
+        paired(step)
+
+    @pl.loop(0, 8)
+    def _(i):
+        @pl.when(i == 5)
+        def _():
+            passed_on(4)
+
+        @pl.when(i == 7)
+        def _():
+            paired(4)
+        forward(lax.rem(z + 8 + (1 - 2 * (i % 2)) * ((i + 1) // 2), 8), HALO, SPAN)
     got(halo_rows, sh.at[0], rh.at[0])
     first = jnp.logical_and(z == 0, core == 0)
     halo = xbuf[HALO - 64:HALO, :]
@@ -230,13 +256,7 @@
 
     @pl.loop(0, 8)
     def _(c):
-        w = wbuf[pl.ds(pl.multiple_of(c * 256, 256), 256), :]
-
-        @pl.loop(0, 4)
-        def _(i):
-            part = lax.dot_general(xbuf[pl.ds(pl.multiple_of(64 + 400 * i, 16), 400), :], w, (((1,), (1,)), ((), ())),
-                                   preferred_element_type=F32)
-            acc[pl.ds(pl.multiple_of(400 * i + 8 * c, 8), 400), :] += part
+        forward(c, HALO - 64, 64)
 
     cbuf[...] = acc[48:1600, 0:128] + acc[44:1596, 128:256]
     ubuf[...] = cbuf[8:1552, :] + pltpu.roll(cbuf[6:1550, :], 64, 1)
@@ -262,12 +282,27 @@
         if step > (0 if early else 1):
             got(gr.at[way, step - 1, sub], sg.at[way, step - 1, sub], rg.at[way, step - 1, sub])
             own = own + gr[way, step - 1, sub].astype(F32)
+        if step == 3:
+            deliver(way, sub, own)
+            return
         gs[way, step, sub] = own.astype(BF)
-        return send(gs.at[way, step, sub], gr.at[way, step, sub], sg.at[way, step, sub], rg.at[way, step, sub],
-                    along(1 if way == 0 else -1))
-
-    @pl.loop(0, 8)
-    def _(pos):
+        send(gs.at[way, step, sub], gr.at[way, step, sub], sg.at[way, step, sub], rg.at[way, step, sub],
+             along(1 if way == 0 else -1)).start()
+
+    def delivery(n, sub, j):
+        cols = pl.ds(128 * sub, 128)
+        return (fs.at[n, pl.ds(32 * j, 32), cols], fr.at[n, pl.ds(pl.multiple_of(32 * x, 32), 32), cols], sf.at[n, sub, j],
+                rf.at[n, sub, x], spread(j, (1, -1, 0)[n]))
+
+    def deliver(n, sub, part):
+        fs[n, :, 128 * sub:128 * (sub + 1)] = part.T.astype(BF)
+        for j in range(4):
+            if n < 2:
+                send(*delivery(n, sub, j)).start()
+            else:
+                go_any(*delivery(n, sub, j))
+
+    def correlate(pos):
         m = (pos + 1) // 2
         zc = lax.rem(z + 8 + (4 - m) * (2 * (pos % 2) - 1), 8)
         odd = zc % 2
@@ -277,38 +312,50 @@
         dall[pos, 1] = part[:, 128:256]
         dxs[pos] = dall[pos, 1 - core].astype(BF)
         send(dxs.at[pos], dxr.at[pos], sdx.at[pos], rdx.at[pos], partner).start()
-        for step in range(4):
-            @pl.when(pos == 2 * step)
+
+    def ring_step(step):
+        for at in ((2 * step - 1, 2 * step) if step else (0,)):
+            got(dxr.at[at], sdx.at[at], rdx.at[at])
+        for n in (0, 1) if step == 0 else (2, 3, 0, 1) if step == 1 else range(4):
+            way, subs = ways[n]
+            for sub in subs:
+                ring_add(step, way, sub)
+
+    @pl.loop(0, 4)
+    def _(pos):
+        correlate(pos)
+        for step in range(2):
+            @pl.when(pos == 2 * step + 1)
             def _():
-                for at in ((2 * step - 1, 2 * step) if step else (0,)):
-                    got(dxr.at[at], sdx.at[at], rdx.at[at])
-                for n, (way, subs) in enumerate(ways):
-                    if step or n < 2:
-                        for sub in subs:
-                            ring_add(step, way, sub).start()
+                ring_step(step)
 
     back = rp[HALO:HALO + SPAN, :].T
     for j in range(4):
         rsend[j] = back[0:32, 384 * j:384 * (j + 1)].astype(BF)
         go_any(rsend.at[j], rrecv.at[pl.ds(pl.multiple_of(32 * x, 32), 32)], so.at[j], ro.at[x], spread(j))
-    for j in range(4):
-        got(rrecv.at[pl.ds(32 * j, 32)], so.at[j], ro.at[j])
-    res_ref[...] = rrecv[...].astype(F32).T.astype(BF)
-
+
+    @pl.loop(4, 8)
+    def _(pos):
+        correlate(pos)
+
+        @pl.when(pos == 5)
+        def _():
+            ring_step(2)
     got(dxr.at[7], sdx.at[7], rdx.at[7])
     for sub in range(4):
         rows = pl.ds(128 * sub, 128)
-        whole = dall[7, core, rows, :] + dxr[7, rows, :].astype(F32)
-        for way in range(2):
-            got(gr.at[way, 3, sub], sg.at[way, 3, sub], rg.at[way, 3, sub])
-            whole = whole + gr[way, 3, sub].astype(F32)
-        fs[:, 128 * sub:128 * (sub + 1)] = whole.T.astype(BF)
-    for j in range(4):
-        go_any(fs.at[pl.ds(32 * j, 32)], fr.at[pl.ds(pl.multiple_of(32 * x, 32), 32)], sf.at[j], rf.at[x], spread(j))
-    for j in range(4):
-        rows = pl.ds(32 * j, 32)
-        got(fr.at[rows], sf.at[j], rf.at[j])
-        new_ref[rows, :] = par_ref[rows, :] + fr[rows, :].astype(F32) * (0.5 / math.sqrt(24576))
+        deliver(2, sub, dall[7, core, rows, :] + dxr[7, rows, :].astype(F32))
+    for j in range(4):
+        got(rrecv.at[pl.ds(32 * j, 32)], so.at[j], ro.at[j])
+    res_ref[...] = rrecv[...].astype(F32).T.astype(BF)
+    ring_step(3)
+    for sub in range(4):
+        cols = pl.ds(128 * sub, 128)
+        for n in (2, 0, 1):
+            for j in range(4):
+                got(fr.at[n, pl.ds(32 * j, 32), cols], sf.at[n, sub, j], rf.at[n, sub, j])
+        total = fr[0, :, cols].astype(F32) + fr[1, :, cols].astype(F32) + fr[2, :, cols].astype(F32)
+        new_ref[:, cols] = par_ref[:, cols] + total * (0.5 / math.sqrt(24576))
 
     for wait in sent:
         wait()
@@ -316,7 +363,11 @@
     @pl.loop(0, 8)
     def _(pos):
         send(dxs.at[pos], dxr.at[pos], sdx.at[pos], rdx.at[pos], partner).wait_send()
-    for step in range(4):
+    for way in range(2):
+        for sub in range(4):
+            for j in range(4):
+                send(*delivery(way, sub, j)).wait_send()
+    for step in range(3):
         for n, (way, subs) in enumerate(ways):
             if step or n < 2:
                 for sub in subs:
@@ -354,14 +405,14 @@
             pltpu.VMEM((8, 2, 512, 128), F32),
             pltpu.VMEM((8, 512, 128), BF),
             pltpu.VMEM((8, 512, 128), BF),
-            pltpu.VMEM((2, 4, 4, 128, 128), BF),
-            pltpu.VMEM((2, 4, 4, 128, 128), BF),
-            pltpu.VMEM((128, 512), BF),
-            pltpu.VMEM((128, 512), BF),
+            pltpu.VMEM((2, 3, 4, 128, 128), BF),
+            pltpu.VMEM((2, 3, 4, 128, 128), BF),
+            pltpu.VMEM((3, 128, 512), BF),
+            pltpu.VMEM((3, 128, 512), BF),
             dma((4,)), dma((4,)), dma((4,)), dma((4, 3)), dma((2, 3)), dma((16,)), dma((4,)), dma((4,)), dma((4,)), dma((4,)),
             dma((4,)), dma((4,)), dma((1,)), dma((1,)),
             dma((2, 4, 4)), dma((2, 4, 4)), dma((8, 4)), dma((8, 4)),
-            dma((8,)), dma((8,)), dma((2, 4, 4)), dma((2, 4, 4)), dma((4,)), dma((4,)),
+            dma((8,)), dma((8,)), dma((2, 3, 4)), dma((2, 3, 4)), dma((3, 4, 4)), dma((3, 4, 4)),
         ],
         compiler_params=pltpu.CompilerParams(collective_id=0, has_side_effects=True, vmem_limit_bytes=56 * 1024 * 1024),
         name="gradient_step",

time: 75.8 us -> 69.8 us (0.921)
  Pallas kernels: 72.1 us -> 66 us
    pallas_call x1, Pallas kernels: 72.1 us -> 66 us  [on_device(): pl.pallas_call(body, out_shape=(jax.ShapeDtypeStruct((128, 512), F32), ja...]
where the time goes in v3:
time: 69.8 us; the launch traced here: 69.7 us
  Pallas kernels  66 us (95%)
  local copies, waits for them, and re-layouts  2.35 us (3%)
  between operations  1.29 us (2%)
    pallas_call x1, Pallas kernels, on_device(): pl.pallas_call(body, out_shape=(jax.ShapeDtypeStruct((128, 512), F32), ja...  66 us
    unnamed x4, local copies, waits for them, and re-layouts  2.35 us

profile of v3, /device:TPU:1, one launch (start us, length us, event | category | flops | bytes accessed | tf_op | source)
XLA Modules:
  0.0 69.7 jit_solution(953290551418149166)
XLA Ops:
  1.3 66.0 %gradient_step.1 = (f32[128,512]{1,0:T(8,128)}, bf16[384,128]{1,0:T(8,128)(2,1)}) custom-call(s32[1]{0:T(128)S(6)} %copy.8.len_ref, bf16[384,128]{1,0:T(8,128)(2,1)} %rec_ref.1, bf16[384,128]{1,0:T(8,128)(2,1)} %meas_ref.1, f32[128,512]{1,0:T(8,128)} %bitcast.2), custom_call_target="tpu_custom_call" | custom-call | tf_op jit(solution)/shard_map/gradient_step/pallas_call | solution.py:380
  67.3 0.0 copy-start
  67.3 1.7 %copy.9 = f32[1,128,512]{2,1,0:T(8,128)} copy(f32[1,128,512]{2,1,0:T(8,128)} %bitcast.3) | data formatting | bytes 524288
  69.0 0.0 copy-done
  69.0 0.6 copy.10
Async XLA Ops:
  67.3 1.7 %copy-start = (bf16[384,128]{1,0:T(8,128)(2,1)S(1)}, bf16[384,128]{1,0:T(8,128)(2,1)}, u32[]{:S(2)}) copy-start(bf16[384,128]{1,0:T(8,128)(2,1)} %get-tuple-element.9) | copy-start | bytes 294916

commit v4 on v3

--- a/solution.py
+++ b/solution.py
@@ -117,7 +117,7 @@
         return wbuf.at[pl.ds(pl.multiple_of(lax.rem(chunk + 8, 8) * 256 + half * 128 + sub * 32, 32), 32)]
 
     def slot(g, j):
-        return xbuf.at[pl.ds(pl.multiple_of(HALO + 384 * j, 128), 384), pl.ds(pl.multiple_of(128 * g, 128), 128)]
+        return xbuf.at[g, pl.ds(pl.multiple_of(HALO + 384 * j, 128), 384)]
 
     for j in range(4):
         go_any(wsend.at[pl.ds(32 * j, 32)], lag_rows(z, yh, x), sb1.at[j], rb1.at[x], spread(j))
@@ -128,7 +128,7 @@
     for j in range(4):
         go_any(msend.at[pl.ds(32 * j, 32)], mrecv.at[x], sm.at[j], rm.at[x], spread(j))
         go_any(lsend, lraw.at[x], sl.at[j], rl.at[x], spread(j))
-    xbuf[0:64, :] = jnp.zeros((64, 512), BF)
+    xbuf[:, 0:64, :] = jnp.zeros((4, 64, 128), BF)
     mtf[32:128, :] = jnp.zeros((96, SPAN), F32)
     rp[...] = jnp.zeros_like(rp)
     acc[...] = jnp.zeros_like(acc)
@@ -159,8 +159,11 @@
     for sub in range(4):
         got(lag_rows(z, core, sub), sb1.at[sub], rb1.at[sub])
         ring_send(0, 0, sub)
+        if sub >= 2:
+            ring_send(1, 0, sub)
+        pair_send(0, 0, sub)
+    for sub in range(2):
         ring_send(1, 0, sub)
-        pair_send(0, 0, sub)
 
     def slot_got(g, j):
         got(slot(g, j), sa.at[0], ra.at[g * 4 + j])
@@ -168,12 +171,13 @@
     def turned(g, j):
         cols = pl.ds(pl.multiple_of(HALO + 384 * j, 128), 384)
         rows = pl.ds(pl.multiple_of(128 * g, 128), 128)
-        xt[rows, cols] = xbuf[cols, rows].T
+        xt[rows, cols] = xbuf[g, cols, :].T
 
     for n in range(2):
-        g = 2 * n + 1
-        slot_got(g, x)
-        for k in (1, 2, 3):
+        slot_got(2 * n + 1, x)
+    for k in (2, 1, 3):
+        for n in range(2):
+            g = 2 * n + 1
             go(slot(g, x), slot(g, x), sb2.at[n, k - 1], ra.at[g * 4 + x], over_x(k))
     for n in range(4):
         j = lax.rem(x + 4 - n, 4)
@@ -181,7 +185,7 @@
         @pl.when(home)
         def _():
             slot_got(yl * 2, j)
-        for k in (1, 2, 3):
+        for k in (2, 1, 3):
             go(slot(yl * 2, j), slot(yl * 2, j), sa2.at[n, k - 1], ra.at[yl * 8 + j], over_y(k), home)
 
     def arrived(n):
@@ -214,11 +218,11 @@
             for sub in subs:
                 pair_got(number(way, step), z - step if way == 0 else z + step, sub)
 
-    halo_rows = xbuf.at[pl.ds(HALO - 64, 64)]
-    last_rows = xbuf.at[pl.ds(HALO + SPAN - 64, 64)]
+    halo_rows = xbuf.at[:, pl.ds(HALO - 64, 64)]
+    last_rows = xbuf.at[:, pl.ds(HALO + SPAN - 64, 64)]
 
     def forward(c, lo, rows):
-        part = lax.dot_general(xbuf[lo:lo + rows, :], wbuf[pl.ds(pl.multiple_of(c * 256, 256), 256), :],
+        part = lax.dot_general(jnp.concatenate([xbuf[g, lo:lo + rows, :] for g in range(4)], 1), wbuf[pl.ds(pl.multiple_of(c * 256, 256), 256), :],
                                (((1,), (1,)), ((), ())), preferred_element_type=F32)
         acc[pl.ds(pl.multiple_of(lo - 64 + 8 * c, 8), rows), :] += part
 
@@ -237,7 +241,20 @@
     for step in range(1, 4):
         paired(step)
 
-    @pl.loop(0, 8)
+    def chunk(i):
+        return lax.rem(z + 8 + (1 - 2 * (i % 2)) * ((i + 1) // 2), 8)
+
+    @pl.loop(0, 4)
+    def _(i):
+        forward(chunk(i), HALO, SPAN)
+    got(halo_rows, sh.at[0], rh.at[0])
+    first = jnp.logical_and(z == 0, core == 0)
+    for g in range(4):
+        halo = xbuf[g, HALO - 64:HALO, :]
+        xbuf[g, HALO - 64:HALO, :] = jnp.where(first, jnp.zeros_like(halo), halo)
+        xt[128 * g:128 * (g + 1), 0:HALO] = xbuf[g, 0:HALO, :].T
+
+    @pl.loop(4, 8)
     def _(i):
         @pl.when(i == 5)
         def _():
@@ -246,17 +263,11 @@
         @pl.when(i == 7)
         def _():
             paired(4)
-        forward(lax.rem(z + 8 + (1 - 2 * (i % 2)) * ((i + 1) // 2), 8), HALO, SPAN)
-    got(halo_rows, sh.at[0], rh.at[0])
-    first = jnp.logical_and(z == 0, core == 0)
-    halo = xbuf[HALO - 64:HALO, :]
-    halo = jnp.where(first, jnp.zeros_like(halo), halo)
-    xbuf[HALO - 64:HALO, :] = halo
-    xt[:, 0:HALO] = xbuf[0:HALO, :].T
-
-    @pl.loop(0, 8)
-    def _(c):
-        forward(c, HALO - 64, 64)
+        forward(chunk(i), HALO - 64, SPAN + 64)
+
+    @pl.loop(0, 4)
+    def _(i):
+        forward(chunk(i), HALO - 64, 64)
 
     cbuf[...] = acc[48:1600, 0:128] + acc[44:1596, 128:256]
     ubuf[...] = cbuf[8:1552, :] + pltpu.roll(cbuf[6:1550, :], 64, 1)
@@ -290,12 +301,11 @@
              along(1 if way == 0 else -1)).start()
 
     def delivery(n, sub, j):
-        cols = pl.ds(128 * sub, 128)
-        return (fs.at[n, pl.ds(32 * j, 32), cols], fr.at[n, pl.ds(pl.multiple_of(32 * x, 32), 32), cols], sf.at[n, sub, j],
+        return (fs.at[n, sub, pl.ds(32 * j, 32)], fr.at[n, sub, pl.ds(pl.multiple_of(32 * x, 32), 32)], sf.at[n, sub, j],
                 rf.at[n, sub, x], spread(j, (1, -1, 0)[n]))
 
     def deliver(n, sub, part):
-        fs[n, :, 128 * sub:128 * (sub + 1)] = part.T.astype(BF)
+        fs[n, sub] = part.T.astype(BF)
         for j in range(4):
             if n < 2:
                 send(*delivery(n, sub, j)).start()
@@ -316,7 +326,7 @@
     def ring_step(step):
         for at in ((2 * step - 1, 2 * step) if step else (0,)):
             got(dxr.at[at], sdx.at[at], rdx.at[at])
-        for n in (0, 1) if step == 0 else (2, 3, 0, 1) if step == 1 else range(4):
+        for n in (2, 3, 0, 1) if step else (0, 1):
             way, subs = ways[n]
             for sub in subs:
                 ring_add(step, way, sub)
@@ -353,8 +363,8 @@
         cols = pl.ds(128 * sub, 128)
         for n in (2, 0, 1):
             for j in range(4):
-                got(fr.at[n, pl.ds(32 * j, 32), cols], sf.at[n, sub, j], rf.at[n, sub, j])
-        total = fr[0, :, cols].astype(F32) + fr[1, :, cols].astype(F32) + fr[2, :, cols].astype(F32)
+                got(fr.at[n, sub, pl.ds(32 * j, 32)], sf.at[n, sub, j], rf.at[n, sub, j])
+        total = fr[0, sub].astype(F32) + fr[1, sub].astype(F32) + fr[2, sub].astype(F32)
         new_ref[:, cols] = par_ref[:, cols] + total * (0.5 / math.sqrt(24576))
 
     for wait in sent:
@@ -385,7 +395,7 @@
         scratch_shapes=[
             pltpu.VMEM((128, 512), BF),
             pltpu.VMEM((2048, 512), BF),
-            pltpu.VMEM((HALO + SPAN, 512), BF),
+            pltpu.VMEM((4, HALO + SPAN, 128), BF),
             pltpu.VMEM((512, HALO + SPAN), BF),
             pltpu.VMEM((128, 384), BF),
             pltpu.VMEM((4, 32, 384), BF),
@@ -407,14 +417,14 @@
             pltpu.VMEM((8, 512, 128), BF),
             pltpu.VMEM((2, 3, 4, 128, 128), BF),
             pltpu.VMEM((2, 3, 4, 128, 128), BF),
-            pltpu.VMEM((3, 128, 512), BF),
-            pltpu.VMEM((3, 128, 512), BF),
+            pltpu.VMEM((3, 4, 128, 128), BF),
+            pltpu.VMEM((3, 4, 128, 128), BF),
             dma((4,)), dma((4,)), dma((4,)), dma((4, 3)), dma((2, 3)), dma((16,)), dma((4,)), dma((4,)), dma((4,)), dma((4,)),
             dma((4,)), dma((4,)), dma((1,)), dma((1,)),
             dma((2, 4, 4)), dma((2, 4, 4)), dma((8, 4)), dma((8, 4)),
             dma((8,)), dma((8,)), dma((2, 3, 4)), dma((2, 3, 4)), dma((3, 4, 4)), dma((3, 4, 4)),
         ],
-        compiler_params=pltpu.CompilerParams(collective_id=0, has_side_effects=True, vmem_limit_bytes=56 * 1024 * 1024),
+        compiler_params=pltpu.CompilerParams(collective_id=0, has_side_effects=True, vmem_limit_bytes=34 * 1024 * 1024),
         name="gradient_step",
     )(seg_lengths, records, measured, markov_params.reshape(128, 512))
     return new.reshape(1, 128, 512), res

time: 69.8 us -> 67 us (0.960)
  Pallas kernels: 66 us -> 61.4 us
  local copies, waits for them, and re-layouts: 2.35 us -> 4.07 us
    pallas_call x1, Pallas kernels: 66 us -> 61.4 us  [on_device(): pl.pallas_call(body, out_shape=(jax.ShapeDtypeStruct((128, 512), F32), ja...]
    unnamed x4 -> x8, local copies, waits for them, and re-layouts: 2.35 us -> 4.07 us
where the time goes in v4:
time: 67 us; the launch traced here: 66.8 us
  Pallas kernels  61.4 us (92%)
  local copies, waits for them, and re-layouts  4.07 us (6%)
  between operations  1.3 us (2%)
    pallas_call x1, Pallas kernels, on_device(): pl.pallas_call(body, out_shape=(jax.ShapeDtypeStruct((128, 512), F32), ja...  61.4 us
    unnamed x8, local copies, waits for them, and re-layouts  4.07 us

profile of v4, /device:TPU:1, one launch (start us, length us, event | category | flops | bytes accessed | tf_op | source)
XLA Modules:
  0.0 66.8 jit_solution(4529573469209819110)
XLA Ops:
  1.3 0.0 copy-start
  1.3 0.9 %copy-done = f32[1,128,512]{2,1,0:T(8,128)S(1)} copy-done((f32[1,128,512]{2,1,0:T(8,128)S(1)}, f32[1,128,512]{2,1,0:T(8,128)}, u32[]{:S(2)}) %copy-start) | copy-done | bytes 262168
  2.2 0.0 copy-start.1
  2.2 0.9 %copy-done.1 = bf16[384,128]{1,0:T(8,128)(2,1)S(1)} copy-done((bf16[384,128]{1,0:T(8,128)(2,1)S(1)}, bf16[384,128]{1,0:T(8,128)(2,1)}, u32[]{:S(2)}) %copy-start.1) | copy-done | bytes 98328
  3.1 0.0 copy-start.2
  3.1 0.9 %copy-done.2 = bf16[384,128]{1,0:T(8,128)(2,1)S(1)} copy-done((bf16[384,128]{1,0:T(8,128)(2,1)S(1)}, bf16[384,128]{1,0:T(8,128)(2,1)}, u32[]{:S(2)}) %copy-start.2) | copy-done | bytes 98328
  4.0 61.4 %gradient_step.1 = (f32[128,512]{1,0:T(8,128)S(1)}, bf16[384,128]{1,0:T(8,128)(2,1)S(1)}) custom-call(s32[1]{0:T(128)S(6)} %copy.8.len_ref, bf16[384,128]{1,0:T(8,128)(2,1)S(1)} %copy-done.1, bf16[384,128]{1,0:T(8,128)(2,1)S(1)} %copy-done.2, f32[128,512]{1,0:T(8,128)S(1)} %bitcast.2), custom_call_target="tpu_custom_call" | custom-call | tf_op jit(solution)/shard_map/gradient_step/pallas_call | solution.py:390
  65.5 0.7 %copy.9 = f32[1,128,512]{2,1,0:T(8,128)} copy(f32[1,128,512]{2,1,0:T(8,128)S(1)} %bitcast.3) | data formatting | bytes 524288
  66.2 0.6 copy.10
Async XLA Ops:
  1.3 1.0 %copy-start = (f32[1,128,512]{2,1,0:T(8,128)S(1)}, f32[1,128,512]{2,1,0:T(8,128)}, u32[]{:S(2)}) copy-start(f32[1,128,512]{2,1,0:T(8,128)} %param.6) | copy-start | bytes 786436
  2.2 0.9 %copy-start.1 = (bf16[384,128]{1,0:T(8,128)(2,1)S(1)}, bf16[384,128]{1,0:T(8,128)(2,1)}, u32[]{:S(2)}) copy-start(bf16[384,128]{1,0:T(8,128)(2,1)} %rec_ref.1) | copy-start | bytes 294916
  3.1 0.9 %copy-start.2 = (bf16[384,128]{1,0:T(8,128)(2,1)S(1)}, bf16[384,128]{1,0:T(8,128)(2,1)}, u32[]{:S(2)}) copy-start(bf16[384,128]{1,0:T(8,128)(2,1)} %meas_ref.1) | copy-start | bytes 294916

commit v5 on v4

--- a/solution.py
+++ b/solution.py
@@ -15,7 +15,7 @@
 SPAN = 1536
 
 
-def body(len_ref, rec_ref, meas_ref, par_ref, new_ref, res_ref, wsend, wbuf, xbuf, xt, msend, mrecv, mtf, mtime, lsend,
+def body(len_ref, rec_ref, meas_hbm, par_hbm, new_ref, res_ref, meas_ref, par_ref, sin, wsend, wbuf, xbuf, xt, msend, mrecv, mtf, mtime, lsend,
          lraw, acc, cbuf, ubuf, rp, wq, qq, qs, rsend, rrecv, dall, dxs, dxr, gs, gr, fs, fr,
          sb1, rb1, sa, sa2, sb2, ra, sm, rm, sl, rl, so, ro, sh, rh, sring, rring, spair, rpair, sdx, rdx, sg, rg, sf, rf):
     tm = lax.axis_index("tm")
@@ -94,6 +94,10 @@
     def got(dst, ssem, rsem):
         send(dst, dst, ssem, rsem, partner).wait_recv()
 
+    loads = [pltpu.make_async_copy(par_hbm, par_ref, sin.at[0]), pltpu.make_async_copy(meas_hbm, meas_ref, sin.at[1])]
+    for load in loads:
+        load.start()
+
     barrier = pltpu.get_barrier_semaphore()
     count = jnp.int32(0)
     friends = [(spread(j, dz), True) for dz in (1, -1) for j in range(4)] + [(spread(j), True) for j in range(4)] + [(first_hop(j), True) for j in range(4)]
@@ -109,6 +113,7 @@
     sure += [along(1), along(-1), partner, ahead, behind]
     for dev in sure:
         pl.semaphore_signal(barrier, inc=1, **where(dev))
+    loads[0].wait()
     wsend[...] = par_ref[...].astype(BF)
     lsend[...] = jnp.full((8, 128), len_ref[0], jnp.int32).astype(F32)
     pl.semaphore_wait(barrier, count + len(sure))
@@ -124,6 +129,7 @@
     for j in range(4):
         go_any(rec_ref, slot(grp, x), sa.at[j], ra.at[grp * 4 + x], first_hop(j))
 
+    loads[1].wait()
     msend[...] = meas_ref[...].astype(F32).T.astype(BF)
     for j in range(4):
         go_any(msend.at[pl.ds(32 * j, 32)], mrecv.at[x], sm.at[j], rm.at[x], spread(j))
@@ -390,9 +396,12 @@
     new, res = pl.pallas_call(
         body,
         out_shape=(jax.ShapeDtypeStruct((128, 512), F32), jax.ShapeDtypeStruct((384, 128), BF)),
-        in_specs=[pl.BlockSpec(memory_space=pltpu.SMEM)] + [pl.BlockSpec(memory_space=pltpu.VMEM)] * 3,
+        in_specs=[pl.BlockSpec(memory_space=pltpu.SMEM)] + [pl.BlockSpec(memory_space=pltpu.HBM)] * 3,
         out_specs=(pl.BlockSpec(memory_space=pltpu.VMEM), pl.BlockSpec(memory_space=pltpu.VMEM)),
         scratch_shapes=[
+            pltpu.VMEM((384, 128), BF),
+            pltpu.VMEM((128, 512), F32),
+            dma((2,)),
             pltpu.VMEM((128, 512), BF),
             pltpu.VMEM((2048, 512), BF),
             pltpu.VMEM((4, HALO + SPAN, 128), BF),
@@ -426,7 +435,7 @@
         ],
         compiler_params=pltpu.CompilerParams(collective_id=0, has_side_effects=True, vmem_limit_bytes=34 * 1024 * 1024),
         name="gradient_step",
-    )(seg_lengths, records, measured, markov_params.reshape(128, 512))
+    )(seg_lengths, *(pltpu.with_memory_space_constraint(a, pltpu.HBM) for a in (records, measured, markov_params.reshape(128, 512))))
     return new.reshape(1, 128, 512), res
 
 

time: 67 us -> 64.6 us (0.964)
  local copies, waits for them, and re-layouts: 4.07 us -> 1.35 us
    unnamed x8 -> x2, local copies, waits for them, and re-layouts: 4.07 us -> 1.35 us
where the time goes in v5:
time: 64.6 us; the launch traced here: 64.5 us
  Pallas kernels  61.8 us (96%)
  local copies, waits for them, and re-layouts  1.35 us (2%)
  between operations  1.29 us (2%)
    pallas_call x1, Pallas kernels, on_device(): pl.pallas_call(body, out_shape=(jax.ShapeDtypeStruct((128, 512), F32), ja...  61.8 us
    unnamed x2, local copies, waits for them, and re-layouts  1.35 us

profile of v5, /device:TPU:1, one launch (start us, length us, event | category | flops | bytes accessed | tf_op | source)
XLA Modules:
  0.0 64.5 jit_solution(12688907596259263815)
XLA Ops:
  1.3 61.8 %gradient_step.1 = (f32[128,512]{1,0:T(8,128)S(1)}, bf16[384,128]{1,0:T(8,128)(2,1)S(1)}) custom-call(s32[1]{0:T(128)S(6)} %copy.8.len_ref, bf16[384,128]{1,0:T(8,128)(2,1)} %rec_ref.1, bf16[384,128]{1,0:T(8,128)(2,1)} %meas_hbm.1, f32[128,512]{1,0:T(8,128)} %bitcast.3), custom_call_target="tpu_custom_call" | custom-call | tf_op jit(solution)/shard_map/gradient_step/pallas_call | solution.py:396
  63.1 0.7 %copy.9 = f32[1,128,512]{2,1,0:T(8,128)} copy(f32[1,128,512]{2,1,0:T(8,128)S(1)} %bitcast.2) | data formatting | bytes 524288
  63.8 0.6 copy.10

commit v6 on v5

--- a/solution.py
+++ b/solution.py
@@ -131,9 +131,6 @@
 
     loads[1].wait()
     msend[...] = meas_ref[...].astype(F32).T.astype(BF)
-    for j in range(4):
-        go_any(msend.at[pl.ds(32 * j, 32)], mrecv.at[x], sm.at[j], rm.at[x], spread(j))
-        go_any(lsend, lraw.at[x], sl.at[j], rl.at[x], spread(j))
     xbuf[:, 0:64, :] = jnp.zeros((4, 64, 128), BF)
     mtf[32:128, :] = jnp.zeros((96, SPAN), F32)
     rp[...] = jnp.zeros_like(rp)
@@ -193,6 +190,10 @@
             slot_got(yl * 2, j)
         for k in (2, 1, 3):
             go(slot(yl * 2, j), slot(yl * 2, j), sa2.at[n, k - 1], ra.at[yl * 8 + j], over_y(k), home)
+
+    for j in range(4):
+        go_any(msend.at[pl.ds(32 * j, 32)], mrecv.at[x], sm.at[j], rm.at[x], spread(j))
+        go_any(lsend, lraw.at[x], sl.at[j], rl.at[x], spread(j))
 
     def arrived(n):
         j = lax.rem(x + 4 - n, 4)
@@ -234,11 +235,6 @@
 
     for step in range(1, 4):
         passed_on(step)
-    for j in range(4):
-        got(mrecv.at[j], sm.at[j], rm.at[j])
-        got(lraw.at[j], sl.at[j], rl.at[j])
-        mtf[0:32, 384 * j:384 * (j + 1)] = mrecv[j].astype(F32)
-    mtime[...] = mtf[...].T
     for n in range(4):
         arrived(n)
     go(last_rows, halo_rows, sh.at[0], rh.at[0], ahead)
@@ -253,6 +249,11 @@
     @pl.loop(0, 4)
     def _(i):
         forward(chunk(i), HALO, SPAN)
+    for j in range(4):
+        got(mrecv.at[j], sm.at[j], rm.at[j])
+        got(lraw.at[j], sl.at[j], rl.at[j])
+        mtf[0:32, 384 * j:384 * (j + 1)] = mrecv[j].astype(F32)
+    mtime[...] = mtf[...].T
     got(halo_rows, sh.at[0], rh.at[0])
     first = jnp.logical_and(z == 0, core == 0)
     for g in range(4):

time: 64.6 us -> 63.6 us (0.985)
  Pallas kernels: 61.8 us -> 60.8 us
    pallas_call x1, Pallas kernels: 61.8 us -> 60.8 us  [on_device(): pl.pallas_call(body, out_shape=(jax.ShapeDtypeStruct((128, 512), F32), ja...]
where the time goes in v6:
time: 63.6 us; the launch traced here: 63.4 us
  Pallas kernels  60.8 us (96%)
  local copies, waits for them, and re-layouts  1.35 us (2%)
  between operations  1.29 us (2%)
    pallas_call x1, Pallas kernels, on_device(): pl.pallas_call(body, out_shape=(jax.ShapeDtypeStruct((128, 512), F32), ja...  60.8 us
    unnamed x2, local copies, waits for them, and re-layouts  1.35 us

profile of v6, /device:TPU:1, one launch (start us, length us, event | category | flops | bytes accessed | tf_op | source)
XLA Modules:
  0.0 63.4 jit_solution(528763560254694004)
XLA Ops:
  1.3 60.8 %gradient_step.1 = (f32[128,512]{1,0:T(8,128)S(1)}, bf16[384,128]{1,0:T(8,128)(2,1)S(1)}) custom-call(s32[1]{0:T(128)S(6)} %copy.8.len_ref, bf16[384,128]{1,0:T(8,128)(2,1)} %rec_ref.1, bf16[384,128]{1,0:T(8,128)(2,1)} %meas_hbm.1, f32[128,512]{1,0:T(8,128)} %bitcast.3), custom_call_target="tpu_custom_call" | custom-call | tf_op jit(solution)/shard_map/gradient_step/pallas_call | solution.py:397
  62.1 0.7 %copy.9 = f32[1,128,512]{2,1,0:T(8,128)} copy(f32[1,128,512]{2,1,0:T(8,128)S(1)} %bitcast.2) | data formatting | bytes 524288
  62.8 0.6 %copy.10 = bf16[384,128]{1,0:T(8,128)(2,1)} copy(bf16[384,128]{1,0:T(8,128)(2,1)S(1)} %get-tuple-element.9) | data formatting | bytes 196608
